TPU v7x, 32 devices: a whole 2x2x4 slice. The times are simulated.
32 devices in a mesh: cand: 4 (over x, core), seq: 8 (over z, y).
Axes of the slice: x: 2, y: 2, z: 4, core: 2. Of those that a mesh axis runs over, the one named last changes fastest.
Arguments:
- response_query_array: bfloat16 [8, 768, 2560], P('cand', 'seq'), may hold values from -180 to 180
- response_key_array: bfloat16 [8, 768, 512], P('cand', 'seq'), may hold values from -6 to 6
- response_value_array: bfloat16 [8, 768, 512], P('cand', 'seq'), may hold values from -6 to 6
- prompt_key_array: bfloat16 [2048, 512], P(('cand', 'seq')), may hold values from -6 to 6
- prompt_value_array: bfloat16 [2048, 512], P(('cand', 'seq')), may hold values from -6 to 6
- lengths: int32 [8], replicated, may hold values from 192 to 768, as said below
- offsets: int32 [8], replicated, may hold values from 512 to 2048, as said below
- ranks: int32 [8], replicated, may hold values from 0 to 7, each once
Outputs:
- attention: bfloat16 [8, 768, 2560], P('cand', 'seq')
Inputs may be any that keep to these rules, and one draw needn't show every extreme that they name: `lengths`: some candidate's response has all 768 positions live. `offsets`: some candidate sees the whole prompt.
All inputs are finite; a program needn't handle non-finite values.
Results may differ from a plain program's by a relative error of at most 0.004.
Values may be sent and summed in bfloat16 or wider, within the bound.
No kernel may reach another device: no remote copies, remote signals or barrier semaphores. Data moves between devices by JAX's collectives and lax.ppermute only.
A program may use at most 128 MiB of HBM per device.

v0:
```python
import math
import jax
import jax.numpy as jnp
from jax import lax
from jax.sharding import PartitionSpec as P

QUERY_HEADS = 20
KEY_VALUE_HEADS = 4
HEAD_DIMENSION = 128
lowest_score_value = -1e30


def attend_block(running, query_rows, block_keys, block_values, allowed, shared):
    running_max, running_total, running_sum = running
    cand_count = query_rows.shape[0]
    heads_kv = query_rows.shape[2]
    head_size = query_rows.shape[4]
    score_scale = 1.0 / math.sqrt(head_size)
    if shared:
        keys_split = block_keys.reshape(block_keys.shape[0], heads_kv, head_size)
        values_split = block_values.reshape(block_values.shape[0], heads_kv, head_size)
        scores = jnp.einsum(
            "crhgd,nhd->chgrn", query_rows, keys_split, preferred_element_type=jnp.float32
        )
    else:
        keys_split = block_keys.reshape(cand_count, block_keys.shape[1], heads_kv, head_size)
        values_split = block_values.reshape(cand_count, block_values.shape[1], heads_kv, head_size)
        scores = jnp.einsum(
            "crhgd,cnhd->chgrn", query_rows, keys_split, preferred_element_type=jnp.float32
        )
    scores = jnp.where(allowed[:, None, None, :, :], scores * score_scale, -jnp.inf)
    new_max = jnp.maximum(running_max, jnp.max(scores, axis=-1))
    rescale = jnp.exp(running_max - new_max)
    exponent = jnp.exp(scores - new_max[..., None])
    weights = exponent.astype(jnp.bfloat16)
    new_total = running_total * rescale + jnp.sum(exponent, axis=-1)
    if shared:
        contrib = jnp.einsum(
            "chgrn,nhd->chgrd", weights, values_split, preferred_element_type=jnp.float32
        )
    else:
        contrib = jnp.einsum(
            "chgrn,cnhd->chgrd", weights, values_split, preferred_element_type=jnp.float32
        )
    new_sum = running_sum * rescale[..., None] + contrib
    return (new_max, new_total, new_sum)


def fold_blocks(
    running, query_rows, all_keys, all_values, key_pos, allowed_of, shared, live_of=None
):
    key_count = key_pos.shape[0]
    block_len = math.gcd(key_count, 512)
    keys_axis = 0 if shared else 1

    def one_block(step_at, carried):
        block_start = step_at * block_len
        block_keys = lax.dynamic_slice_in_dim(all_keys, block_start, block_len, keys_axis)
        block_values = lax.dynamic_slice_in_dim(all_values, block_start, block_len, keys_axis)
        block_pos = lax.dynamic_slice_in_dim(key_pos, block_start, block_len, 0)
        return attend_block(
            carried, query_rows, block_keys, block_values, allowed_of(block_pos), shared
        )

    return lax.fori_loop(0, key_count // block_len, one_block, running)


def body(
    response_query_array,
    response_key_array,
    response_value_array,
    prompt_key_array,
    prompt_value_array,
    lengths,
    offsets,
    ranks,
):
    candidate_local, output_rows, width = response_query_array.shape
    group_width = QUERY_HEADS // KEY_VALUE_HEADS
    group_at = lax.axis_index("cand")
    seq_at = lax.axis_index("seq")
    first_cand = group_at * candidate_local
    my_lengths = lax.dynamic_slice_in_dim(lengths, first_cand, candidate_local)
    my_offsets = lax.dynamic_slice_in_dim(offsets, first_cand, candidate_local)
    query_pos = seq_at * output_rows + jnp.arange(output_rows, dtype=jnp.int32)
    query_rows = response_query_array.reshape(
        candidate_local, output_rows, KEY_VALUE_HEADS, group_width, HEAD_DIMENSION
    )
    pieces = (
        lax.all_gather(prompt_key_array, ("cand", "seq"), axis=0, tiled=True),
        lax.all_gather(prompt_value_array, ("cand", "seq"), axis=0, tiled=True),
    )
    key_pos = jnp.arange(pieces[0].shape[0], dtype=jnp.int32)

    def allowed_of(block_pos):
        return block_pos[None, None, :] < my_offsets[:, None, None]

    running = fold_blocks(
        (
            jnp.full(
                (candidate_local, KEY_VALUE_HEADS, group_width, output_rows),
                lowest_score_value,
                jnp.float32,
            ),
            jnp.zeros((candidate_local, KEY_VALUE_HEADS, group_width, output_rows), jnp.float32),
            jnp.zeros(
                (candidate_local, KEY_VALUE_HEADS, group_width, output_rows, HEAD_DIMENSION),
                jnp.float32,
            ),
        ),
        query_rows,
        pieces[0],
        pieces[1],
        key_pos,
        allowed_of,
        True,
    )
    pieces = (
        lax.all_gather(response_key_array, "seq", axis=1, tiled=True),
        lax.all_gather(response_value_array, "seq", axis=1, tiled=True),
    )
    key_pos = jnp.arange(pieces[0].shape[1], dtype=jnp.int32)

    def allowed_of(block_pos):
        causal = block_pos[None, None, :] <= query_pos[None, :, None]
        return causal & (block_pos[None, None, :] < my_lengths[:, None, None])

    final_max, final_total, final_sum = fold_blocks(
        running, query_rows, pieces[0], pieces[1], key_pos, allowed_of, False
    )
    attended = final_sum / final_total[..., None]
    attended = jnp.transpose(attended, (0, 3, 1, 2, 4)).reshape(candidate_local, output_rows, width)
    row_valid = query_pos[None, :] < my_lengths[:, None]
    attended = jnp.where(row_valid[:, :, None], attended, 0.0).astype(jnp.bfloat16)
    gathered = lax.all_gather(attended, "cand", axis=0, tiled=True)
    every_cand = jnp.arange(gathered.shape[0], dtype=jnp.int32)
    chosen = []
    for within in range(candidate_local):
        target = first_cand + within
        source = jnp.sum(jnp.where(ranks == target, every_cand, 0))
        chosen.append(lax.dynamic_index_in_dim(gathered, source, 0, keepdims=False))
    return jnp.stack(chosen, axis=0)


def solution(mesh):
    in_specs = (
        P("cand", "seq", None),
        P("cand", "seq", None),
        P("cand", "seq", None),
        P(("cand", "seq"), None),
        P(("cand", "seq"), None),
        P(),
        P(),
        P(),
    )
    out_specs = P("cand", "seq", None)
    return jax.shard_map(body, mesh=mesh, in_specs=in_specs, out_specs=out_specs, check_vma=False)
```

profile of v0, /device:TPU:0, one launch (start us, length us, event | category | flops | bytes accessed | tf_op | source)
XLA Modules:
  0.0 304.9 jit_solution(10088347945177968936)
XLA Ops:
  6.5 0.7 all-gather.6.cloned.1.call-update
  7.3 0.7 all-gather.8.cloned.1.call-update
  8.1 1.8 copy.56
  9.9 1.8 copy.57
  11.9 1.7 copy.52
  13.6 0.7 copy.54
  14.3 1.4 copy.62
  15.9 53.7 %all-gather.6.cloned.1.call-done = bf16[2048,512]{1,0:T(8,128)(2,1)} async-done(((bf16[64,512]{1,0:T(8,128)(2,1)}), bf16[2048,512]{1,0:T(8,128)(2,1)}) %all-gather.6.cloned.1.call-update) | async-done | bytes 2097168 | tf_op jit(solution)/shard_map/all_gather | solution.py:90
  69.6 58.4 %all-gather.8.cloned.1.call-done = bf16[2048,512]{1,0:T(8,128)(2,1)} async-done(((bf16[64,512]{1,0:T(8,128)(2,1)}), bf16[2048,512]{1,0:T(8,128)(2,1)}) %all-gather.8.cloned.1.call-update) | async-done | bytes 2097168 | tf_op jit(solution)/shard_map/all_gather | solution.py:91
  128.0 65.4 %while.37 = (s32[]{:T(128)}, f32[2,4,5,96]{3,2,0,1:T(8,128)S(1)}, f32[2,4,5,96]{3,2,0,1:T(8,128)S(1)}, f32[2,4,5,96,128]{4,3,2,0,1:T(8,128)}, s32[2048]{0:T(1024...) while((s32[]{:T(128)}, f32[2,4,5,96]{3,2,0,1:T(8,128)S(1)}, ...), condition=%wide.region_3.4_spmd.clone, body=%wide.region_0.3_spmd.clone.sunk | while | flops 1029754624 | bytes 34007236 | solution.py:65
  128.1 1.3 constant_dynamic-slice_fusion.9
  129.6 4.2 %fusion.60 = (f32[2,4,5,96]{3,2,0,1:T(8,128)S(1)}, f32[4,512,2,96,5]{1,3,4,2,0:T(8,128)}) fusion(pred[2,512]{1,0:T(4,128)(4,1)S(1)} %broadcast_compare_fusion.9, bf16[512,4,128,1,1]{0,2,4,3,1:T(8,128)(2,1)S(1)} %bitcast.88, bf16[2,96,4,5,128]{4,1,3,0,2:T(8,128)(2,1)S(1)} %get-tuple-element.683), kind=kOutput, calls=%fused_computation.26.clone.1 | convolution fusion | flops 509210880 | bytes 9388032 | tf_op jit(solution)/shard_map/while/body/eval_jaxpr/crhgd,nhd->chgrn/dot_general | solution.py:22
  133.9 4.5 %fusion.61 = f32[2,4,5,96]{3,2,0,1:T(8,128)S(1)} fusion(f32[4,512,2,96,5]{1,3,4,2,0:T(8,128)} %get-tuple-element.646, f32[2,4,5,96]{3,2,0,1:T(8,128)S(1)} %select_maximum_fusion.2, pred[2,512]{1,0:T(4,128)(4,1)S(1)} %broadcast_compare_fusion.9), kind=kLoop, calls=%fused_computation.25.clone.1 | loop fusion | flops 7860480 | bytes 7896064 | tf_op jit(solution)/shard_map/while/body/eval_jaxpr/reduce_sum | solution.py:36
  138.6 5.4 %bitcast_add_fusion.2 = f32[2,4,5,96,128]{4,3,2,0,1:T(8,128)} fusion(f32[2,4,5,96,128]{4,3,2,0,1:T(8,128)} %get-tuple-element.666, bf16[512,4,128,1,1]{0,2,4,3,1:T(8,128)(2,1)S(1)} %bitcast.91, f32[4,512,2,96,5]{1,3,4,2,0:T(8,128)} %get-tuple-element.646, f32[2,4,5,96]{3,2,0,1:T(8,128)S(1)} %select_maximum_fusion.2, ...), kind=kOutput, calls=%fused_computation.32.clone.1 | convolution fusion | flops 512655360 | bytes 12352513 | tf_op jit(solution)/shard_map/while/body/eval_jaxpr/chgrn,nhd->chgrd/dot_general | solution.py:38
  144.2 1.3 constant_dynamic-slice_fusion.9
  145.7 4.2 %fusion.60 = (f32[2,4,5,96]{3,2,0,1:T(8,128)S(1)}, f32[4,512,2,96,5]{1,3,4,2,0:T(8,128)}) fusion(pred[2,512]{1,0:T(4,128)(4,1)S(1)} %broadcast_compare_fusion.9, bf16[512,4,128,1,1]{0,2,4,3,1:T(8,128)(2,1)S(1)} %bitcast.88, bf16[2,96,4,5,128]{4,1,3,0,2:T(8,128)(2,1)S(1)} %get-tuple-element.683), kind=kOutput, calls=%fused_computation.26.clone.1 | convolution fusion | flops 509210880 | bytes 9388032 | tf_op jit(solution)/shard_map/while/body/eval_jaxpr/crhgd,nhd->chgrn/dot_general | solution.py:22
  149.9 4.4 %fusion.61 = f32[2,4,5,96]{3,2,0,1:T(8,128)S(1)} fusion(f32[4,512,2,96,5]{1,3,4,2,0:T(8,128)} %get-tuple-element.646, f32[2,4,5,96]{3,2,0,1:T(8,128)S(1)} %select_maximum_fusion.2, pred[2,512]{1,0:T(4,128)(4,1)S(1)} %broadcast_compare_fusion.9), kind=kLoop, calls=%fused_computation.25.clone.1 | loop fusion | flops 7860480 | bytes 7896064 | tf_op jit(solution)/shard_map/while/body/eval_jaxpr/reduce_sum | solution.py:36
  154.6 6.0 %bitcast_add_fusion.2 = f32[2,4,5,96,128]{4,3,2,0,1:T(8,128)} fusion(f32[2,4,5,96,128]{4,3,2,0,1:T(8,128)} %get-tuple-element.666, bf16[512,4,128,1,1]{0,2,4,3,1:T(8,128)(2,1)S(1)} %bitcast.91, f32[4,512,2,96,5]{1,3,4,2,0:T(8,128)} %get-tuple-element.646, f32[2,4,5,96]{3,2,0,1:T(8,128)S(1)} %select_maximum_fusion.2, ...), kind=kOutput, calls=%fused_computation.32.clone.1 | convolution fusion | flops 512655360 | bytes 12352513 | tf_op jit(solution)/shard_map/while/body/eval_jaxpr/chgrn,nhd->chgrd/dot_general | solution.py:38
  160.7 1.3 constant_dynamic-slice_fusion.9
  162.2 4.2 %fusion.60 = (f32[2,4,5,96]{3,2,0,1:T(8,128)S(1)}, f32[4,512,2,96,5]{1,3,4,2,0:T(8,128)}) fusion(pred[2,512]{1,0:T(4,128)(4,1)S(1)} %broadcast_compare_fusion.9, bf16[512,4,128,1,1]{0,2,4,3,1:T(8,128)(2,1)S(1)} %bitcast.88, bf16[2,96,4,5,128]{4,1,3,0,2:T(8,128)(2,1)S(1)} %get-tuple-element.683), kind=kOutput, calls=%fused_computation.26.clone.1 | convolution fusion | flops 509210880 | bytes 9388032 | tf_op jit(solution)/shard_map/while/body/eval_jaxpr/crhgd,nhd->chgrn/dot_general | solution.py:22
  166.4 4.4 %fusion.61 = f32[2,4,5,96]{3,2,0,1:T(8,128)S(1)} fusion(f32[4,512,2,96,5]{1,3,4,2,0:T(8,128)} %get-tuple-element.646, f32[2,4,5,96]{3,2,0,1:T(8,128)S(1)} %select_maximum_fusion.2, pred[2,512]{1,0:T(4,128)(4,1)S(1)} %broadcast_compare_fusion.9), kind=kLoop, calls=%fused_computation.25.clone.1 | loop fusion | flops 7860480 | bytes 7896064 | tf_op jit(solution)/shard_map/while/body/eval_jaxpr/reduce_sum | solution.py:36
  171.1 5.9 %bitcast_add_fusion.2 = f32[2,4,5,96,128]{4,3,2,0,1:T(8,128)} fusion(f32[2,4,5,96,128]{4,3,2,0,1:T(8,128)} %get-tuple-element.666, bf16[512,4,128,1,1]{0,2,4,3,1:T(8,128)(2,1)S(1)} %bitcast.91, f32[4,512,2,96,5]{1,3,4,2,0:T(8,128)} %get-tuple-element.646, f32[2,4,5,96]{3,2,0,1:T(8,128)S(1)} %select_maximum_fusion.2, ...), kind=kOutput, calls=%fused_computation.32.clone.1 | convolution fusion | flops 512655360 | bytes 12352513 | tf_op jit(solution)/shard_map/while/body/eval_jaxpr/chgrn,nhd->chgrd/dot_general | solution.py:38
  177.1 1.3 constant_dynamic-slice_fusion.9
  178.6 4.2 %fusion.60 = (f32[2,4,5,96]{3,2,0,1:T(8,128)S(1)}, f32[4,512,2,96,5]{1,3,4,2,0:T(8,128)}) fusion(pred[2,512]{1,0:T(4,128)(4,1)S(1)} %broadcast_compare_fusion.9, bf16[512,4,128,1,1]{0,2,4,3,1:T(8,128)(2,1)S(1)} %bitcast.88, bf16[2,96,4,5,128]{4,1,3,0,2:T(8,128)(2,1)S(1)} %get-tuple-element.683), kind=kOutput, calls=%fused_computation.26.clone.1 | convolution fusion | flops 509210880 | bytes 9388032 | tf_op jit(solution)/shard_map/while/body/eval_jaxpr/crhgd,nhd->chgrn/dot_general | solution.py:22
  182.8 4.4 %fusion.61 = f32[2,4,5,96]{3,2,0,1:T(8,128)S(1)} fusion(f32[4,512,2,96,5]{1,3,4,2,0:T(8,128)} %get-tuple-element.646, f32[2,4,5,96]{3,2,0,1:T(8,128)S(1)} %select_maximum_fusion.2, pred[2,512]{1,0:T(4,128)(4,1)S(1)} %broadcast_compare_fusion.9), kind=kLoop, calls=%fused_computation.25.clone.1 | loop fusion | flops 7860480 | bytes 7896064 | tf_op jit(solution)/shard_map/while/body/eval_jaxpr/reduce_sum | solution.py:36
  187.5 5.9 %bitcast_add_fusion.2 = f32[2,4,5,96,128]{4,3,2,0,1:T(8,128)} fusion(f32[2,4,5,96,128]{4,3,2,0,1:T(8,128)} %get-tuple-element.666, bf16[512,4,128,1,1]{0,2,4,3,1:T(8,128)(2,1)S(1)} %bitcast.91, f32[4,512,2,96,5]{1,3,4,2,0:T(8,128)} %get-tuple-element.646, f32[2,4,5,96]{3,2,0,1:T(8,128)S(1)} %select_maximum_fusion.2, ...), kind=kOutput, calls=%fused_computation.32.clone.1 | convolution fusion | flops 512655360 | bytes 12352513 | tf_op jit(solution)/shard_map/while/body/eval_jaxpr/chgrn,nhd->chgrd/dot_general | solution.py:38
  193.4 1.7 copy.60
  195.1 0.6 copy.58
  195.7 0.6 copy.59
  196.3 22.1 %all-gather.12.cloned.1.call-done = bf16[2,768,512]{2,0,1:T(2,128)(2,1)} async-done(((bf16[2,96,512]{2,0,1:T(2,128)(2,1)}), bf16[2,768,512]{2,0,1:T(2,128)(2,1)}) %all-gather.12.cloned.1.call-update) | async-done | bytes 1572880 | tf_op jit(solution)/shard_map/all_gather | solution.py:120
  218.4 41.8 %while.36 = (s32[]{:T(128)}, f32[2,4,5,96]{3,2,1,0:T(8,128)}, f32[2,4,5,96]{3,2,1,0:T(8,128)}, f32[2,4,5,96,128]{4,3,2,1,0:T(8,128)S(1)}, s32[768]{0:T(1024)S(1)...) while((s32[]{:T(128)}, f32[2,4,5,96]{3,2,1,0:T(8,128)}, ...), condition=%wide.region_7.8_spmd.clone, body=%wide.region_4.7_spmd.clone.sunk | while | flops 515194976 | bytes 38561872 | solution.py:65
  218.6 0.7 broadcast_and_fusion.2
  219.3 1.9 constant_dynamic-slice_fusion.8
  221.2 0.5 copy.86
  221.8 2.2 fusion.54
  224.0 1.8 copy-done
  225.9 1.5 fusion.55
  227.5 0.5 copy.87
  228.0 3.7 %multiply_add_fusion.5 = f32[2,4,5,96,128]{4,3,2,1,0:T(8,128)S(1)} fusion(f32[2,4,5,96,128]{4,3,2,1,0:T(8,128)S(1)} %get-tuple-element.706, bf16[2,256,4,128,1]{1,3,4,2,0:T(8,128)(2,1)S(1)} %bitcast.89, f32[2,4,256,96,5]{2,3,4,1,0:T(8,128)} %copy-done, f32[2,4,5,96]{3,2,1,0:T(8,128)S(1)} %max.19, pred[2,96,256]{2,1,0:T(8,128)(4,1)S(1)} %copy-done.1, ...), kind=kOutput, calls=%fused_computation.7.clone.1 | convolution fusion | flops 256573440 | bytes 8468480 | tf_op jit(solution)/shard_map/while/body/eval_jaxpr/chgrn,cnhd->chgrd/dot_general | solution.py:42
  231.7 0.6 copy.111
  232.6 0.7 broadcast_and_fusion.2
  233.2 1.9 constant_dynamic-slice_fusion.8
  235.2 0.5 copy.86
  235.7 2.2 fusion.54
  238.0 1.8 copy-done
  239.8 1.5 fusion.55
  241.9 3.7 %multiply_add_fusion.5 = f32[2,4,5,96,128]{4,3,2,1,0:T(8,128)S(1)} fusion(f32[2,4,5,96,128]{4,3,2,1,0:T(8,128)S(1)} %get-tuple-element.706, bf16[2,256,4,128,1]{1,3,4,2,0:T(8,128)(2,1)S(1)} %bitcast.89, f32[2,4,256,96,5]{2,3,4,1,0:T(8,128)} %copy-done, f32[2,4,5,96]{3,2,1,0:T(8,128)S(1)} %max.19, pred[2,96,256]{2,1,0:T(8,128)(4,1)S(1)} %copy-done.1, ...), kind=kOutput, calls=%fused_computation.7.clone.1 | convolution fusion | flops 256573440 | bytes 8468480 | tf_op jit(solution)/shard_map/while/body/eval_jaxpr/chgrn,cnhd->chgrd/dot_general | solution.py:42
  245.6 0.6 copy.111
  246.5 0.7 broadcast_and_fusion.2
  247.2 1.9 constant_dynamic-slice_fusion.8
  249.1 0.5 copy.86
  249.7 2.2 fusion.54
  251.9 1.8 copy-done
  253.7 1.5 fusion.55
  255.9 3.7 %multiply_add_fusion.5 = f32[2,4,5,96,128]{4,3,2,1,0:T(8,128)S(1)} fusion(f32[2,4,5,96,128]{4,3,2,1,0:T(8,128)S(1)} %get-tuple-element.706, bf16[2,256,4,128,1]{1,3,4,2,0:T(8,128)(2,1)S(1)} %bitcast.89, f32[2,4,256,96,5]{2,3,4,1,0:T(8,128)} %copy-done, f32[2,4,5,96]{3,2,1,0:T(8,128)S(1)} %max.19, pred[2,96,256]{2,1,0:T(8,128)(4,1)S(1)} %copy-done.1, ...), kind=kOutput, calls=%fused_computation.7.clone.1 | convolution fusion | flops 256573440 | bytes 8468480 | tf_op jit(solution)/shard_map/while/body/eval_jaxpr/chgrn,cnhd->chgrd/dot_general | solution.py:42
  259.6 0.6 copy.111
  260.2 1.3 divide_bitcast_fusion
  261.5 0.8 copy.64
  262.3 0.6 copy.65
  262.9 1.2 select_convert_fusion
  264.2 0.7 fusion.29
  268.5 27.6 %all-gather.14.cloned.1.call-done = bf16[8,96,2560]{2,1,0:T(8,128)(2,1)} async-done(((bf16[2,96,2560]{2,1,0:T(8,128)(2,1)}), bf16[8,96,2560]{2,1,0:T(8,128)(2,1)}) %all-gather.14.cloned.1.call-update) | async-done | bytes 3932176 | tf_op jit(solution)/shard_map/all_gather | solution.py:135
  296.1 1.2 constant_dynamic-slice_fusion.5
  297.3 1.0 pad_maximum_fusion
  (99 shorter events, 4.9 us)
Async XLA Ops:
  6.5 63.1 %all-gather.6.cloned.1.call-start = ((), (), s32[]{:S(2)}) async-start(), calls=%async_computation | async-start | bytes 2162688 | tf_op jit(solution)/shard_map/all_gather | solution.py:90
  7.3 120.7 %all-gather.8.cloned.1.call-start = ((), (), s32[]{:S(2)}) async-start(), calls=%async_computation.1 | async-start | bytes 2162688 | tf_op jit(solution)/shard_map/all_gather | solution.py:91
  8.0 188.3 %all-gather.10.cloned.1.call-start = ((), (), s32[]{:S(2)}) async-start(), calls=%async_computation.2 | async-start | bytes 1769472 | tf_op jit(solution)/shard_map/all_gather | solution.py:119
  9.9 5.8 %copy-start.6 = (s32[8]{0:T(128)S(1)}, s32[8]{0:T(128)}, u32[]{:S(2)}) copy-start(s32[8]{0:T(128)} %param.18) | copy-start | bytes 100
  9.9 5.9 %copy-start.7 = (s32[8]{0:T(128)S(1)}, s32[8]{0:T(128)}, u32[]{:S(2)}) copy-start(s32[8]{0:T(128)} %param.17) | copy-start | bytes 100
  9.9 208.5 %all-gather.12.cloned.1.call-start = ((), (), s32[]{:S(2)}) async-start(), calls=%async_computation.3 | async-start | bytes 1769472 | tf_op jit(solution)/shard_map/all_gather | solution.py:120
  11.8 284.3 %all-gather.14.cloned.1.call-start = ((), (), s32[]{:S(2)}) async-start(), calls=%async_computation.4 | async-start | bytes 4915200 | tf_op jit(solution)/shard_map/all_gather | solution.py:135
  221.8 2.2 copy-start.2
  221.8 4.1 %copy-start.1 = (pred[2,96,256]{2,1,0:T(8,128)(4,1)S(1)}, pred[2,96,256]{2,1,0:T(8,128)(4,1)}, u32[]{:S(2)}) copy-start(pred[2,96,256]{2,1,0:T(8,128)(4,1)} %broadcast_and_fusion.2) | copy-start | bytes 147460 | tf_op jit(solution)/shard_map/while
  221.8 5.6 %copy-start.3 = (f32[2,4,5,96]{3,2,1,0:T(8,128)S(1)}, f32[2,4,5,96]{3,2,1,0:T(8,128)}, u32[]{:S(2)}) copy-start(f32[2,4,5,96]{3,2,1,0:T(8,128)} %get-tuple-element.705) | copy-start | bytes 46084 | tf_op jit(solution)/shard_map/while
  224.0 1.8 copy-start
  227.4 4.3 %copy-start.4 = (f32[2,4,5,96]{3,2,1,0:T(8,128)}, f32[2,4,5,96]{3,2,1,0:T(8,128)S(1)}, u32[]{:S(2)}) copy-start(f32[2,4,5,96]{3,2,1,0:T(8,128)S(1)} %get-tuple-element.719) | copy-start | bytes 46084 | tf_op jit(solution)/shard_map/while
  235.7 2.2 copy-start.2
  235.7 4.1 %copy-start.1 = (pred[2,96,256]{2,1,0:T(8,128)(4,1)S(1)}, pred[2,96,256]{2,1,0:T(8,128)(4,1)}, u32[]{:S(2)}) copy-start(pred[2,96,256]{2,1,0:T(8,128)(4,1)} %broadcast_and_fusion.2) | copy-start | bytes 147460 | tf_op jit(solution)/shard_map/while
  235.7 5.6 %copy-start.3 = (f32[2,4,5,96]{3,2,1,0:T(8,128)S(1)}, f32[2,4,5,96]{3,2,1,0:T(8,128)}, u32[]{:S(2)}) copy-start(f32[2,4,5,96]{3,2,1,0:T(8,128)} %get-tuple-element.705) | copy-start | bytes 46084 | tf_op jit(solution)/shard_map/while
  237.9 1.8 copy-start
  241.4 4.3 %copy-start.4 = (f32[2,4,5,96]{3,2,1,0:T(8,128)}, f32[2,4,5,96]{3,2,1,0:T(8,128)S(1)}, u32[]{:S(2)}) copy-start(f32[2,4,5,96]{3,2,1,0:T(8,128)S(1)} %get-tuple-element.719) | copy-start | bytes 46084 | tf_op jit(solution)/shard_map/while
  249.6 2.2 copy-start.2
  249.6 4.1 %copy-start.1 = (pred[2,96,256]{2,1,0:T(8,128)(4,1)S(1)}, pred[2,96,256]{2,1,0:T(8,128)(4,1)}, u32[]{:S(2)}) copy-start(pred[2,96,256]{2,1,0:T(8,128)(4,1)} %broadcast_and_fusion.2) | copy-start | bytes 147460 | tf_op jit(solution)/shard_map/while
  249.7 5.6 %copy-start.3 = (f32[2,4,5,96]{3,2,1,0:T(8,128)S(1)}, f32[2,4,5,96]{3,2,1,0:T(8,128)}, u32[]{:S(2)}) copy-start(f32[2,4,5,96]{3,2,1,0:T(8,128)} %get-tuple-element.705) | copy-start | bytes 46084 | tf_op jit(solution)/shard_map/while
  251.9 1.8 copy-start
  255.3 4.3 %copy-start.4 = (f32[2,4,5,96]{3,2,1,0:T(8,128)}, f32[2,4,5,96]{3,2,1,0:T(8,128)S(1)}, u32[]{:S(2)}) copy-start(f32[2,4,5,96]{3,2,1,0:T(8,128)S(1)} %get-tuple-element.719) | copy-start | bytes 46084 | tf_op jit(solution)/shard_map/while
  261.5 2.6 copy-start.5
Sparse Core Ops, SparseCore 0:
  10.3 59.2 all-gather.5
  72.6 55.3 all-gather.7
  130.2 43.0 all-gather.9
  175.3 43.0 all-gather.11
  264.3 31.7 all-gather.13
where the time goes:
time: 306 us; the launch traced here: 305 us
  waiting for transfers between devices  163 us (53%)
  matrix products  57.7 us (19%)
  local copies, waits for them, and re-layouts  36.7 us (12%)
  other arithmetic  29.6 us (10%)
  between operations  16.9 us (6%)
    all_gather x1, waiting for transfers between devices, body(): lax.all_gather(prompt_value_array, ('cand', 'seq'), axis=0, tiled=True)  58.4 us
    all_gather x1, waiting for transfers between devices, body(): lax.all_gather(prompt_key_array, ('cand', 'seq'), axis=0, tiled=True)  53.7 us
    all_gather x1, waiting for transfers between devices, body(): gathered = lax.all_gather(attended, 'cand', axis=0, tiled=True)  27.6 us
    dot_general x4, matrix products, attend_block(): jnp.einsum('chgrn,nhd->chgrd', weights, values_split, preferred_element_t...  23.1 us
    reduce_sum x7, other arithmetic, attend_block(): new_total = running_total * rescale + jnp.sum(exponent, axis=-1)  22.3 us
    all_gather x1, waiting for transfers between devices, body(): lax.all_gather(response_value_array, 'seq', axis=1, tiled=True)  22.1 us
    dot_general x4, matrix products, attend_block(): jnp.einsum('crhgd,nhd->chgrn', query_rows, keys_split, preferred_element_...  16.9 us
    dynamic_slice x14, local copies, waits for them, and re-layouts, one_block(): lax.dynamic_slice_in_dim(all_values, block_start, block_len, keys_axis)  13.3 us
  transfers between devices with their start and end apart: 5, of which 4 were waited for; matrix products, arithmetic and copies ran while one was open for 25% of the time, Pallas kernels for 0%

commit v1 on v0

--- a/solution.py
+++ b/solution.py
@@ -8,6 +8,18 @@
 KEY_VALUE_HEADS = 4
 HEAD_DIMENSION = 128
 lowest_score_value = -1e30
+
+
+def gather_by_bits(array, axis, dim):
+    ways, here, hop = (lax.axis_size(axis), lax.axis_index(axis), array.shape[dim])
+    line, have = (array, 1)
+    while have < ways:
+        line = jnp.concatenate(
+            [line, lax.ppermute(line, axis, [(d, (d - have) % ways) for d in range(ways)])],
+            axis=dim,
+        )
+        have = 2 * have
+    return jnp.roll(line, here * hop, axis=dim)
 
 
 def attend_block(running, query_rows, block_keys, block_values, allowed, shared):
@@ -88,7 +100,7 @@
     )
     pieces = (
         lax.all_gather(prompt_key_array, ("cand", "seq"), axis=0, tiled=True),
-        lax.all_gather(prompt_value_array, ("cand", "seq"), axis=0, tiled=True),
+        gather_by_bits(prompt_value_array, ("cand", "seq"), 0),
     )
     key_pos = jnp.arange(pieces[0].shape[0], dtype=jnp.int32)
 

time: 306 us -> 256 us (0.84)
  waiting for transfers between devices: 163 us -> 91.6 us
  local copies, waits for them, and re-layouts: 36.7 us -> 52.4 us
  starting transfers between devices: 0.16 us -> 8.75 us
  matrix products: 57.7 us -> 53.5 us
    all_gather x1 -> x0, waiting for transfers between devices: 58.4 us -> none  [body(): lax.all_gather(prompt_value_array, ('cand', 'seq'), axis=0, tiled=True)]
    ppermute x0 -> x5, waiting for transfers between devices: none -> 54.7 us  [gather_by_bits(): lax.ppermute(line, axis, [(d, (d - have) % ways) for d in range(ways)])]
    all_gather x1, waiting for transfers between devices: 53.7 us -> 0.01 us  [body(): lax.all_gather(prompt_key_array, ('cand', 'seq'), axis=0, tiled=True)]
    all_gather x1, waiting for transfers between devices: 22.1 us -> 8.61 us  [body(): lax.all_gather(response_value_array, 'seq', axis=1, tiled=True)]
    concatenate x0 -> x2, local copies, waits for them, and re-layouts: none -> 9.46 us  [the longest x1 7.51 us: gather_by_bits(): return jnp.roll(line, here * hop, axis=dim)]
    ppermute x0 -> x5, starting transfers between devices: none -> 8.63 us  [gather_by_bits(): lax.ppermute(line, axis, [(d, (d - have) % ways) for d in range(ways)])]
    dynamic_slice x7 -> x11, local copies, waits for them, and re-layouts: 2.48 us -> 6.79 us  [one_block(): lax.dynamic_slice_in_dim(all_keys, block_start, block_len, keys_axis)]
    dot_general x4, matrix products: 23.1 us -> 18.9 us  [attend_block(): jnp.einsum('chgrn,nhd->chgrd', weights, values_split, preferred_element_t...]
  transfers between devices with their start and end apart: 5 -> 9, of which waited for: 4 -> 7; matrix products, arithmetic and copies ran while one was open for 25% -> 35% of each run, Pallas kernels for 0% -> 0%
where the time goes in v1:
time: 256 us; the launch traced here: 254 us
  waiting for transfers between devices  91.6 us (36%)
  matrix products  53.5 us (21%)
  local copies, waits for them, and re-layouts  52.4 us (20%)
  other arithmetic  30.5 us (12%)
  between operations  17 us (7%)
  starting transfers between devices  8.75 us (3%)
    ppermute x5, waiting for transfers between devices, gather_by_bits(): lax.ppermute(line, axis, [(d, (d - have) % ways) for d in range(ways)])  54.7 us
    all_gather x1, waiting for transfers between devices, body(): gathered = lax.all_gather(attended, 'cand', axis=0, tiled=True)  27.5 us
    reduce_sum x7, other arithmetic, attend_block(): new_total = running_total * rescale + jnp.sum(exponent, axis=-1)  22.9 us
    dot_general x4, matrix products, attend_block(): jnp.einsum('chgrn,nhd->chgrd', weights, values_split, preferred_element_t...  18.9 us
    dot_general x4, matrix products, attend_block(): jnp.einsum('crhgd,nhd->chgrn', query_rows, keys_split, preferred_element_...  16.9 us
    dynamic_slice x10, local copies, waits for them, and re-layouts, one_block(): lax.dynamic_slice_in_dim(all_values, block_start, block_len, keys_axis)  11.9 us
    dot_general x3, matrix products, attend_block(): jnp.einsum('chgrn,cnhd->chgrd', weights, values_split, preferred_element_...  11.1 us
    unnamed x19, local copies, waits for them, and re-layouts  9.41 us
  transfers between devices with their start and end apart: 9, of which 7 were waited for; matrix products, arithmetic and copies ran while one was open for 35% of the time, Pallas kernels for 0%

profile of v1, /device:TPU:0, one launch (start us, length us, event | category | flops | bytes accessed | tf_op | source)
XLA Modules:
  0.0 254.4 jit_solution(15693656871667753655)
XLA Ops:
  6.5 0.7 all-gather.5.cloned.1.call-update
  7.3 1.8 copy.74
  9.2 1.0 copy.70
  10.1 6.4 %collective-permute-start = (bf16[64,512]{0,1:T(8,128)(2,1)S(1)}, bf16[64,512]{0,1:T(8,128)(2,1)S(1)}, u32[]{:S(2)}, u32[]{:S(2)}) collective-permute-start(bf16[64,512]{0,1:T(8,128)(2,1)S(1)} %copy.70), channel_id=1, source_target_pairs={{0,31},{1,0},{2,1},{3,2},{4,3},{5,4},{6,5},{7,6},{8,7},{9,8},{10,9... | collective-permute-start | bytes 196616 | tf_op jit(solution)/shard_map/ppermute | solution.py:18
  16.6 2.9 %collective-permute-done = bf16[64,512]{0,1:T(8,128)(2,1)S(1)} collective-permute-done((bf16[64,512]{0,1:T(8,128)(2,1)S(1)}, bf16[64,512]{0,1:T(8,128)(2,1)S(1)}, u32[]{:S(2)}, u32[]{:S(2)}) %collective-permute-start) | collective-permute-done | bytes 65568 | tf_op jit(solution)/shard_map/ppermute | solution.py:18
  20.2 4.6 %collective-permute-done.1 = bf16[128,512]{0,1:T(8,128)(2,1)S(1)} collective-permute-done((bf16[128,512]{0,1:T(8,128)(2,1)S(1)}, bf16[128,512]{0,1:T(8,128)(2,1)S(1)}, u32[]{:S(2)}, u32[]{:S(2)}) %collective-permute-start.1) | collective-permute-done | bytes 131104 | tf_op jit(solution)/shard_map/ppermute | solution.py:18
  24.9 15.4 %collective-permute-done.2 = bf16[256,512]{0,1:T(8,128)(2,1)S(1)} collective-permute-done((bf16[256,512]{0,1:T(8,128)(2,1)S(1)}, bf16[256,512]{0,1:T(8,128)(2,1)S(1)}, u32[]{:S(2)}, u32[]{:S(2)}) %collective-permute-start.2) | collective-permute-done | bytes 262176 | tf_op jit(solution)/shard_map/ppermute | solution.py:18
  40.6 8.5 %collective-permute-done.3 = bf16[512,512]{0,1:T(8,128)(2,1)S(1)} collective-permute-done((bf16[512,512]{0,1:T(8,128)(2,1)S(1)}, bf16[512,512]{0,1:T(8,128)(2,1)S(1)}, u32[]{:S(2)}, u32[]{:S(2)}) %collective-permute-start.3) | collective-permute-done | bytes 524320 | tf_op jit(solution)/shard_map/ppermute | solution.py:18
  49.1 1.9 concatenate.25
  51.1 1.5 collective-permute-start.4
  52.6 0.9 copy.75
  53.6 0.8 copy.64
  54.3 0.7 copy.73
  55.0 1.4 copy.80
  56.6 23.3 %collective-permute-done.4 = bf16[1024,512]{0,1:T(8,128)(2,1)} collective-permute-done((bf16[1024,512]{0,1:T(8,128)(2,1)}, bf16[1024,512]{0,1:T(8,128)(2,1)}, u32[]{:S(2)}, u32[]{:S(2)}) %collective-permute-start.4) | collective-permute-done | bytes 1048608 | tf_op jit(solution)/shard_map/ppermute | solution.py:18
  79.9 7.5 %concatenate.26 = bf16[4096,512]{0,1:T(8,128)(2,1)} concatenate(bf16[64,512]{0,1:T(8,128)(2,1)S(1)} %copy.70, bf16[64,512]{0,1:T(8,128)(2,1)S(1)} %collective-permute-done, bf16[128,512]{0,1:T(8,128)(2,1)S(1)} %collective-permute-done.1, bf16[256,512]{0,1:T(8,128)(2,1)S(1)} %collective-permute-done.2, bf16[512,512]{0,1:T(8,128)(2,1)S(1)} %collective-permute-done.3, ...), dimensions={0} | concatenate | bytes 8388608 | tf_op jit(solution)/shard_map/jit(_roll_dynamic)/concatenate | solution.py:22
  87.4 4.2 %constant_dynamic-slice_fusion.6 = bf16[2048,512]{0,1:T(8,128)(2,1)} fusion(bf16[4096,512]{0,1:T(8,128)(2,1)} %concatenate.26, s32[]{:T(128)S(6)} %select_n.71), kind=kLoop, calls=%fused_computation.53 | loop fusion | bytes 4194308 | tf_op jit(solution)/shard_map/jit(_roll_dynamic)/dynamic_slice | solution.py:22
  91.6 64.7 %while.37 = (s32[]{:T(128)}, f32[2,4,5,96]{3,2,0,1:T(8,128)S(1)}, f32[2,4,5,96]{3,2,0,1:T(8,128)S(1)}, f32[2,4,5,96,128]{4,3,2,0,1:T(8,128)}, s32[2048]{0:T(1024...) while((s32[]{:T(128)}, f32[2,4,5,96]{3,2,0,1:T(8,128)S(1)}, ...), condition=%wide.region_3.4_spmd.clone, body=%wide.region_0.3_spmd.clone.sunk | while | flops 1029754624 | bytes 64415972 | solution.py:77
  91.8 1.1 constant_dynamic-slice_fusion.11
  93.1 4.2 %fusion.60 = (f32[2,4,5,96]{3,2,0,1:T(8,128)S(1)}, f32[4,512,2,96,5]{1,3,4,2,0:T(8,128)}) fusion(pred[2,512]{1,0:T(4,128)(4,1)S(1)} %broadcast_compare_fusion.9, bf16[512,4,128,1,1]{0,2,4,3,1:T(8,128)(2,1)S(1)} %bitcast.88, bf16[2,96,4,5,128]{4,1,3,0,2:T(8,128)(2,1)S(1)} %get-tuple-element.677), kind=kOutput, calls=%fused_computation.26.clone.1 | convolution fusion | flops 509210880 | bytes 9388032 | tf_op jit(solution)/shard_map/while/body/eval_jaxpr/crhgd,nhd->chgrn/dot_general | solution.py:34
  97.3 4.5 %fusion.61 = f32[2,4,5,96]{3,2,0,1:T(8,128)S(1)} fusion(f32[4,512,2,96,5]{1,3,4,2,0:T(8,128)} %get-tuple-element.641, f32[2,4,5,96]{3,2,0,1:T(8,128)S(1)} %select_maximum_fusion.2, pred[2,512]{1,0:T(4,128)(4,1)S(1)} %broadcast_compare_fusion.9), kind=kLoop, calls=%fused_computation.25.clone.1 | loop fusion | flops 7860480 | bytes 7896064 | tf_op jit(solution)/shard_map/while/body/eval_jaxpr/reduce_sum | solution.py:48
  101.9 1.1 constant_dynamic-slice_fusion.12
  102.9 3.7 %bitcast_add_fusion.2 = f32[2,4,5,96,128]{4,3,2,0,1:T(8,128)} fusion(f32[2,4,5,96,128]{4,3,2,0,1:T(8,128)} %get-tuple-element.660, bf16[512,4,128,1,1]{0,2,4,3,1:T(8,128)(2,1)S(1)} %bitcast.91, f32[4,512,2,96,5]{1,3,4,2,0:T(8,128)S(1)} %copy-done, f32[2,4,5,96]{3,2,0,1:T(8,128)S(1)} %select_maximum_fusion.2, ...), kind=kOutput, calls=%fused_computation.32.clone.1 | convolution fusion | flops 512655360 | bytes 12352513 | tf_op jit(solution)/shard_map/while/body/eval_jaxpr/chgrn,nhd->chgrd/dot_general | solution.py:50
  106.8 1.1 constant_dynamic-slice_fusion.11
  108.0 4.2 %fusion.60 = (f32[2,4,5,96]{3,2,0,1:T(8,128)S(1)}, f32[4,512,2,96,5]{1,3,4,2,0:T(8,128)}) fusion(pred[2,512]{1,0:T(4,128)(4,1)S(1)} %broadcast_compare_fusion.9, bf16[512,4,128,1,1]{0,2,4,3,1:T(8,128)(2,1)S(1)} %bitcast.88, bf16[2,96,4,5,128]{4,1,3,0,2:T(8,128)(2,1)S(1)} %get-tuple-element.677), kind=kOutput, calls=%fused_computation.26.clone.1 | convolution fusion | flops 509210880 | bytes 9388032 | tf_op jit(solution)/shard_map/while/body/eval_jaxpr/crhgd,nhd->chgrn/dot_general | solution.py:34
  112.3 4.5 %fusion.61 = f32[2,4,5,96]{3,2,0,1:T(8,128)S(1)} fusion(f32[4,512,2,96,5]{1,3,4,2,0:T(8,128)} %get-tuple-element.641, f32[2,4,5,96]{3,2,0,1:T(8,128)S(1)} %select_maximum_fusion.2, pred[2,512]{1,0:T(4,128)(4,1)S(1)} %broadcast_compare_fusion.9), kind=kLoop, calls=%fused_computation.25.clone.1 | loop fusion | flops 7860480 | bytes 7896064 | tf_op jit(solution)/shard_map/while/body/eval_jaxpr/reduce_sum | solution.py:48
  116.9 1.1 constant_dynamic-slice_fusion.12
  118.0 5.1 %bitcast_add_fusion.2 = f32[2,4,5,96,128]{4,3,2,0,1:T(8,128)} fusion(f32[2,4,5,96,128]{4,3,2,0,1:T(8,128)} %get-tuple-element.660, bf16[512,4,128,1,1]{0,2,4,3,1:T(8,128)(2,1)S(1)} %bitcast.91, f32[4,512,2,96,5]{1,3,4,2,0:T(8,128)S(1)} %copy-done, f32[2,4,5,96]{3,2,0,1:T(8,128)S(1)} %select_maximum_fusion.2, ...), kind=kOutput, calls=%fused_computation.32.clone.1 | convolution fusion | flops 512655360 | bytes 12352513 | tf_op jit(solution)/shard_map/while/body/eval_jaxpr/chgrn,nhd->chgrd/dot_general | solution.py:50
  123.2 1.1 constant_dynamic-slice_fusion.11
  124.5 4.2 %fusion.60 = (f32[2,4,5,96]{3,2,0,1:T(8,128)S(1)}, f32[4,512,2,96,5]{1,3,4,2,0:T(8,128)}) fusion(pred[2,512]{1,0:T(4,128)(4,1)S(1)} %broadcast_compare_fusion.9, bf16[512,4,128,1,1]{0,2,4,3,1:T(8,128)(2,1)S(1)} %bitcast.88, bf16[2,96,4,5,128]{4,1,3,0,2:T(8,128)(2,1)S(1)} %get-tuple-element.677), kind=kOutput, calls=%fused_computation.26.clone.1 | convolution fusion | flops 509210880 | bytes 9388032 | tf_op jit(solution)/shard_map/while/body/eval_jaxpr/crhgd,nhd->chgrn/dot_general | solution.py:34
  128.8 4.7 %fusion.61 = f32[2,4,5,96]{3,2,0,1:T(8,128)S(1)} fusion(f32[4,512,2,96,5]{1,3,4,2,0:T(8,128)} %get-tuple-element.641, f32[2,4,5,96]{3,2,0,1:T(8,128)S(1)} %select_maximum_fusion.2, pred[2,512]{1,0:T(4,128)(4,1)S(1)} %broadcast_compare_fusion.9), kind=kLoop, calls=%fused_computation.25.clone.1 | loop fusion | flops 7860480 | bytes 7896064 | tf_op jit(solution)/shard_map/while/body/eval_jaxpr/reduce_sum | solution.py:48
  133.5 1.1 constant_dynamic-slice_fusion.12
  134.6 5.1 %bitcast_add_fusion.2 = f32[2,4,5,96,128]{4,3,2,0,1:T(8,128)} fusion(f32[2,4,5,96,128]{4,3,2,0,1:T(8,128)} %get-tuple-element.660, bf16[512,4,128,1,1]{0,2,4,3,1:T(8,128)(2,1)S(1)} %bitcast.91, f32[4,512,2,96,5]{1,3,4,2,0:T(8,128)S(1)} %copy-done, f32[2,4,5,96]{3,2,0,1:T(8,128)S(1)} %select_maximum_fusion.2, ...), kind=kOutput, calls=%fused_computation.32.clone.1 | convolution fusion | flops 512655360 | bytes 12352513 | tf_op jit(solution)/shard_map/while/body/eval_jaxpr/chgrn,nhd->chgrd/dot_general | solution.py:50
  139.8 1.1 constant_dynamic-slice_fusion.11
  141.1 4.2 %fusion.60 = (f32[2,4,5,96]{3,2,0,1:T(8,128)S(1)}, f32[4,512,2,96,5]{1,3,4,2,0:T(8,128)}) fusion(pred[2,512]{1,0:T(4,128)(4,1)S(1)} %broadcast_compare_fusion.9, bf16[512,4,128,1,1]{0,2,4,3,1:T(8,128)(2,1)S(1)} %bitcast.88, bf16[2,96,4,5,128]{4,1,3,0,2:T(8,128)(2,1)S(1)} %get-tuple-element.677), kind=kOutput, calls=%fused_computation.26.clone.1 | convolution fusion | flops 509210880 | bytes 9388032 | tf_op jit(solution)/shard_map/while/body/eval_jaxpr/crhgd,nhd->chgrn/dot_general | solution.py:34
  145.4 4.5 %fusion.61 = f32[2,4,5,96]{3,2,0,1:T(8,128)S(1)} fusion(f32[4,512,2,96,5]{1,3,4,2,0:T(8,128)} %get-tuple-element.641, f32[2,4,5,96]{3,2,0,1:T(8,128)S(1)} %select_maximum_fusion.2, pred[2,512]{1,0:T(4,128)(4,1)S(1)} %broadcast_compare_fusion.9), kind=kLoop, calls=%fused_computation.25.clone.1 | loop fusion | flops 7860480 | bytes 7896064 | tf_op jit(solution)/shard_map/while/body/eval_jaxpr/reduce_sum | solution.py:48
  149.9 1.2 constant_dynamic-slice_fusion.12
  151.2 5.1 %bitcast_add_fusion.2 = f32[2,4,5,96,128]{4,3,2,0,1:T(8,128)} fusion(f32[2,4,5,96,128]{4,3,2,0,1:T(8,128)} %get-tuple-element.660, bf16[512,4,128,1,1]{0,2,4,3,1:T(8,128)(2,1)S(1)} %bitcast.91, f32[4,512,2,96,5]{1,3,4,2,0:T(8,128)S(1)} %copy-done, f32[2,4,5,96]{3,2,0,1:T(8,128)S(1)} %select_maximum_fusion.2, ...), kind=kOutput, calls=%fused_computation.32.clone.1 | convolution fusion | flops 512655360 | bytes 12352513 | tf_op jit(solution)/shard_map/while/body/eval_jaxpr/chgrn,nhd->chgrd/dot_general | solution.py:50
  156.3 1.7 copy.78
  159.2 8.6 %all-gather.9.cloned.1.call-done = bf16[2,768,512]{2,0,1:T(2,128)(2,1)} async-done(((bf16[2,96,512]{2,0,1:T(2,128)(2,1)}), bf16[2,768,512]{2,0,1:T(2,128)(2,1)}) %all-gather.9.cloned.1.call-update) | async-done | bytes 1572880 | tf_op jit(solution)/shard_map/all_gather | solution.py:132
  167.9 41.8 %while.36 = (s32[]{:T(128)}, f32[2,4,5,96]{3,2,1,0:T(8,128)}, f32[2,4,5,96]{3,2,1,0:T(8,128)}, f32[2,4,5,96,128]{4,3,2,1,0:T(8,128)S(1)}, s32[768]{0:T(1024)S(1)...) while((s32[]{:T(128)}, f32[2,4,5,96]{3,2,1,0:T(8,128)}, ...), condition=%wide.region_7.8_spmd.clone, body=%wide.region_4.7_spmd.clone.sunk | while | flops 515194976 | bytes 38561872 | solution.py:77
  168.1 0.6 broadcast_and_fusion.2
  168.7 1.9 constant_dynamic-slice_fusion.10
  171.2 2.2 fusion.54
  173.5 1.8 copy-done.1
  175.3 1.5 fusion.55
  177.5 3.7 %multiply_add_fusion.5 = f32[2,4,5,96,128]{4,3,2,1,0:T(8,128)S(1)} fusion(f32[2,4,5,96,128]{4,3,2,1,0:T(8,128)S(1)} %get-tuple-element.700, bf16[2,256,4,128,1]{1,3,4,2,0:T(8,128)(2,1)S(1)} %bitcast.89, f32[2,4,256,96,5]{2,3,4,1,0:T(8,128)} %copy-done.1, f32[2,4,5,96]{3,2,1,0:T(8,128)S(1)} %max.19, pred[2,96,256]{2,1,0:T(8,128)(4,1)S(1)} %copy-done.2, ...), kind=kOutput, calls=%fused_computation.7.clone.1 | convolution fusion | flops 256573440 | bytes 8468480 | tf_op jit(solution)/shard_map/while/body/eval_jaxpr/chgrn,cnhd->chgrd/dot_general | solution.py:54
  182.7 1.9 constant_dynamic-slice_fusion.10
  185.2 2.2 fusion.54
  187.4 1.8 copy-done.1
  189.3 1.5 fusion.55
  191.4 3.7 %multiply_add_fusion.5 = f32[2,4,5,96,128]{4,3,2,1,0:T(8,128)S(1)} fusion(f32[2,4,5,96,128]{4,3,2,1,0:T(8,128)S(1)} %get-tuple-element.700, bf16[2,256,4,128,1]{1,3,4,2,0:T(8,128)(2,1)S(1)} %bitcast.89, f32[2,4,256,96,5]{2,3,4,1,0:T(8,128)} %copy-done.1, f32[2,4,5,96]{3,2,1,0:T(8,128)S(1)} %max.19, pred[2,96,256]{2,1,0:T(8,128)(4,1)S(1)} %copy-done.2, ...), kind=kOutput, calls=%fused_computation.7.clone.1 | convolution fusion | flops 256573440 | bytes 8468480 | tf_op jit(solution)/shard_map/while/body/eval_jaxpr/chgrn,cnhd->chgrd/dot_general | solution.py:54
  196.6 1.9 constant_dynamic-slice_fusion.10
  199.1 2.2 fusion.54
  201.4 1.8 copy-done.1
  203.2 1.5 fusion.55
  205.3 3.7 %multiply_add_fusion.5 = f32[2,4,5,96,128]{4,3,2,1,0:T(8,128)S(1)} fusion(f32[2,4,5,96,128]{4,3,2,1,0:T(8,128)S(1)} %get-tuple-element.700, bf16[2,256,4,128,1]{1,3,4,2,0:T(8,128)(2,1)S(1)} %bitcast.89, f32[2,4,256,96,5]{2,3,4,1,0:T(8,128)} %copy-done.1, f32[2,4,5,96]{3,2,1,0:T(8,128)S(1)} %max.19, pred[2,96,256]{2,1,0:T(8,128)(4,1)S(1)} %copy-done.2, ...), kind=kOutput, calls=%fused_computation.7.clone.1 | convolution fusion | flops 256573440 | bytes 8468480 | tf_op jit(solution)/shard_map/while/body/eval_jaxpr/chgrn,cnhd->chgrd/dot_general | solution.py:54
  209.7 1.3 divide_bitcast_fusion
  211.0 0.8 copy.82
  212.4 1.2 select_convert_fusion
  213.6 0.7 fusion.29
  218.0 27.5 %all-gather.11.cloned.1.call-done = bf16[8,96,2560]{2,1,0:T(8,128)(2,1)} async-done(((bf16[2,96,2560]{2,1,0:T(8,128)(2,1)}), bf16[8,96,2560]{2,1,0:T(8,128)(2,1)}) %all-gather.11.cloned.1.call-update) | async-done | bytes 3932176 | tf_op jit(solution)/shard_map/all_gather | solution.py:147
  245.6 1.2 constant_dynamic-slice_fusion.5
  246.8 1.0 pad_maximum_fusion
  (125 shorter events, 12.2 us)
Async XLA Ops:
  6.5 46.0 %copy-start.7 = (bf16[2,96,512]{2,1,0:T(8,128)(2,1)S(1)}, bf16[2,96,512]{2,1,0:T(8,128)(2,1)}, u32[]{:S(2)}) copy-start(bf16[2,96,512]{2,1,0:T(8,128)(2,1)} %param.14) | copy-start | bytes 589828
  6.5 47.0 %copy-start.6 = (bf16[2,96,2560]{2,1,0:T(8,128)(2,1)S(1)}, bf16[2,96,2560]{2,1,0:T(8,128)(2,1)}, u32[]{:S(2)}) copy-start(bf16[2,96,2560]{2,1,0:T(8,128)(2,1)} %param.12) | copy-start | bytes 2949124
  6.5 85.1 %all-gather.5.cloned.1.call-start = ((), (), s32[]{:S(2)}) async-start(), calls=%async_computation | async-start | bytes 2162688 | tf_op jit(solution)/shard_map/all_gather | solution.py:102
  7.3 152.0 %all-gather.7.cloned.1.call-start = ((), (), s32[]{:S(2)}) async-start(), calls=%async_computation.1 | async-start | bytes 1769472 | tf_op jit(solution)/shard_map/all_gather | solution.py:131
  9.1 158.7 %all-gather.9.cloned.1.call-start = ((), (), s32[]{:S(2)}) async-start(), calls=%async_computation.2 | async-start | bytes 1769472 | tf_op jit(solution)/shard_map/all_gather | solution.py:132
  10.1 9.4 %collective-permute-start = (bf16[64,512]{0,1:T(8,128)(2,1)S(1)}, bf16[64,512]{0,1:T(8,128)(2,1)S(1)}, u32[]{:S(2)}, u32[]{:S(2)}) collective-permute-start(bf16[64,512]{0,1:T(8,128)(2,1)S(1)} %copy.70), channel_id=1, source_target_pairs={{0,31},{1,0},{2,1},{3,2},{4,3},{5,4},{6,5},{7,6},{8,7},{9,8},{10,9... | collective-permute-start | bytes 196616 | tf_op jit(solution)/shard_map/ppermute | solution.py:18
  19.6 5.1 %collective-permute-start.1 = (bf16[128,512]{0,1:T(8,128)(2,1)S(1)}, bf16[128,512]{0,1:T(8,128)(2,1)S(1)}, u32[]{:S(2)}, u32[]{:S(2)}) collective-permute-start(bf16[128,512]{0,1:T(8,128)(2,1)S(1)} %pad_maximum_fusion.3), channel_id=1, source_target_pairs={{0,30},{1,31},{2,0},{3,1},{4,2},{5,3},{6,4},{7,5},{8,6},{9,7},{10,... | collective-permute-start | bytes 393224 | tf_op jit(solution)/shard_map/ppermute | solution.py:18
  24.9 15.4 %collective-permute-start.2 = (bf16[256,512]{0,1:T(8,128)(2,1)S(1)}, bf16[256,512]{0,1:T(8,128)(2,1)S(1)}, u32[]{:S(2)}, u32[]{:S(2)}) collective-permute-start(bf16[256,512]{0,1:T(8,128)(2,1)S(1)} %pad_maximum_fusion.2), channel_id=1, source_target_pairs={{0,28},{1,29},{2,30},{3,31},{4,0},{5,1},{6,2},{7,3},{8,4},{9,5},{1... | collective-permute-start | bytes 786440 | tf_op jit(solution)/shard_map/ppermute | solution.py:18
  40.5 8.7 %collective-permute-start.3 = (bf16[512,512]{0,1:T(8,128)(2,1)S(1)}, bf16[512,512]{0,1:T(8,128)(2,1)S(1)}, u32[]{:S(2)}, u32[]{:S(2)}) collective-permute-start(bf16[512,512]{0,1:T(8,128)(2,1)S(1)} %pad_maximum_fusion.1), channel_id=1, source_target_pairs={{0,24},{1,25},{2,26},{3,27},{4,28},{5,29},{6,30},{7,31},{8,0},{9,1... | collective-permute-start | bytes 1572872 | tf_op jit(solution)/shard_map/ppermute | solution.py:18
  51.1 5.3 %copy-start.9 = (s32[8]{0:T(128)S(1)}, s32[8]{0:T(128)}, u32[]{:S(2)}) copy-start(s32[8]{0:T(128)} %param.18) | copy-start | bytes 100
  51.1 5.4 %copy-start.10 = (s32[8]{0:T(128)S(1)}, s32[8]{0:T(128)}, u32[]{:S(2)}) copy-start(s32[8]{0:T(128)} %param.17) | copy-start | bytes 100
  51.1 28.8 %collective-permute-start.4 = (bf16[1024,512]{0,1:T(8,128)(2,1)}, bf16[1024,512]{0,1:T(8,128)(2,1)}, u32[]{:S(2)}, u32[]{:S(2)}) collective-permute-start(bf16[1024,512]{0,1:T(8,128)(2,1)} %concatenate.25), channel_id=1, source_target_pairs={{0,16},{1,17},{2,18},{3,19},{4,20},{5,21},{6,22},{7,23},{8,24},{9,... | collective-permute-start | bytes 3145736 | tf_op jit(solution)/shard_map/ppermute | solution.py:18
  53.5 192.1 %all-gather.11.cloned.1.call-start = ((), (), s32[]{:S(2)}) async-start(), calls=%async_computation.3 | async-start | bytes 4915200 | tf_op jit(solution)/shard_map/all_gather | solution.py:147
  97.3 5.7 %copy-start = (f32[4,512,2,96,5]{1,3,4,2,0:T(8,128)S(1)}, f32[4,512,2,96,5]{1,3,4,2,0:T(8,128)}, u32[]{:S(2)}) copy-start(f32[4,512,2,96,5]{1,3,4,2,0:T(8,128)} %get-tuple-element.641) | copy-start | bytes 23592964 | tf_op jit(solution)/shard_map/while
  112.3 5.7 %copy-start = (f32[4,512,2,96,5]{1,3,4,2,0:T(8,128)S(1)}, f32[4,512,2,96,5]{1,3,4,2,0:T(8,128)}, u32[]{:S(2)}) copy-start(f32[4,512,2,96,5]{1,3,4,2,0:T(8,128)} %get-tuple-element.641) | copy-start | bytes 23592964 | tf_op jit(solution)/shard_map/while
  128.8 5.8 %copy-start = (f32[4,512,2,96,5]{1,3,4,2,0:T(8,128)S(1)}, f32[4,512,2,96,5]{1,3,4,2,0:T(8,128)}, u32[]{:S(2)}) copy-start(f32[4,512,2,96,5]{1,3,4,2,0:T(8,128)} %get-tuple-element.641) | copy-start | bytes 23592964 | tf_op jit(solution)/shard_map/while
  145.4 5.8 %copy-start = (f32[4,512,2,96,5]{1,3,4,2,0:T(8,128)S(1)}, f32[4,512,2,96,5]{1,3,4,2,0:T(8,128)}, u32[]{:S(2)}) copy-start(f32[4,512,2,96,5]{1,3,4,2,0:T(8,128)} %get-tuple-element.641) | copy-start | bytes 23592964 | tf_op jit(solution)/shard_map/while
  171.2 2.2 copy-start.3
  171.2 4.1 %copy-start.2 = (pred[2,96,256]{2,1,0:T(8,128)(4,1)S(1)}, pred[2,96,256]{2,1,0:T(8,128)(4,1)}, u32[]{:S(2)}) copy-start(pred[2,96,256]{2,1,0:T(8,128)(4,1)} %broadcast_and_fusion.2) | copy-start | bytes 147460 | tf_op jit(solution)/shard_map/while
  171.2 5.6 %copy-start.4 = (f32[2,4,5,96]{3,2,1,0:T(8,128)S(1)}, f32[2,4,5,96]{3,2,1,0:T(8,128)}, u32[]{:S(2)}) copy-start(f32[2,4,5,96]{3,2,1,0:T(8,128)} %get-tuple-element.699) | copy-start | bytes 46084 | tf_op jit(solution)/shard_map/while
  173.5 1.9 copy-start.1
  176.9 4.3 %copy-start.5 = (f32[2,4,5,96]{3,2,1,0:T(8,128)}, f32[2,4,5,96]{3,2,1,0:T(8,128)S(1)}, u32[]{:S(2)}) copy-start(f32[2,4,5,96]{3,2,1,0:T(8,128)S(1)} %get-tuple-element.713) | copy-start | bytes 46084 | tf_op jit(solution)/shard_map/while
  185.1 2.2 copy-start.3
  185.2 4.1 %copy-start.2 = (pred[2,96,256]{2,1,0:T(8,128)(4,1)S(1)}, pred[2,96,256]{2,1,0:T(8,128)(4,1)}, u32[]{:S(2)}) copy-start(pred[2,96,256]{2,1,0:T(8,128)(4,1)} %broadcast_and_fusion.2) | copy-start | bytes 147460 | tf_op jit(solution)/shard_map/while
  185.2 5.6 %copy-start.4 = (f32[2,4,5,96]{3,2,1,0:T(8,128)S(1)}, f32[2,4,5,96]{3,2,1,0:T(8,128)}, u32[]{:S(2)}) copy-start(f32[2,4,5,96]{3,2,1,0:T(8,128)} %get-tuple-element.699) | copy-start | bytes 46084 | tf_op jit(solution)/shard_map/while
  187.4 1.9 copy-start.1
  190.8 4.3 %copy-start.5 = (f32[2,4,5,96]{3,2,1,0:T(8,128)}, f32[2,4,5,96]{3,2,1,0:T(8,128)S(1)}, u32[]{:S(2)}) copy-start(f32[2,4,5,96]{3,2,1,0:T(8,128)S(1)} %get-tuple-element.713) | copy-start | bytes 46084 | tf_op jit(solution)/shard_map/while
  199.1 2.2 copy-start.3
  199.1 4.1 %copy-start.2 = (pred[2,96,256]{2,1,0:T(8,128)(4,1)S(1)}, pred[2,96,256]{2,1,0:T(8,128)(4,1)}, u32[]{:S(2)}) copy-start(pred[2,96,256]{2,1,0:T(8,128)(4,1)} %broadcast_and_fusion.2) | copy-start | bytes 147460 | tf_op jit(solution)/shard_map/while
  199.1 5.6 %copy-start.4 = (f32[2,4,5,96]{3,2,1,0:T(8,128)S(1)}, f32[2,4,5,96]{3,2,1,0:T(8,128)}, u32[]{:S(2)}) copy-start(f32[2,4,5,96]{3,2,1,0:T(8,128)} %get-tuple-element.699) | copy-start | bytes 46084 | tf_op jit(solution)/shard_map/while
  201.3 1.9 copy-start.1
  204.8 4.3 %copy-start.5 = (f32[2,4,5,96]{3,2,1,0:T(8,128)}, f32[2,4,5,96]{3,2,1,0:T(8,128)S(1)}, u32[]{:S(2)}) copy-start(f32[2,4,5,96]{3,2,1,0:T(8,128)S(1)} %get-tuple-element.713) | copy-start | bytes 46084 | tf_op jit(solution)/shard_map/while
  211.0 2.6 %copy-start.8 = (s32[8]{0:T(128)S(1)}, s32[8]{0:T(128)}, u32[]{:S(2)}) copy-start(s32[8]{0:T(128)} %param.19) | copy-start | bytes 100
Sparse Core Ops, SparseCore 0:
  10.3 66.9 all-gather.4
  79.5 43.0 all-gather.6
  124.8 42.9 all-gather.8
  213.7 31.7 all-gather.10
